TPU v7x, 32 devices: a whole 2x2x4 slice. The times are simulated.
32 devices in a mesh: path: 8 (over z, x), shard: 4 (over y, core).
Axes of the slice: x: 2, y: 2, z: 4, core: 2. Of those that a mesh axis runs over, the one named last changes fastest.
Arguments:
- master: float32 [2, 4096, 2048], P(None, ('path', 'shard')), may hold values from -6 to 6
- momentum: float32 [2, 4096, 2048], P(None, ('path', 'shard')), may hold values from -2 to 2
- routes: int32 [8, 1], replicated, may hold values from 0 to 1
- counts: int32 [8], replicated, may hold values from 1 to 8
- tokens: bfloat16 [12288, 4096], P(('path', 'shard')), may hold values from -6 to 6
- cotangent: bfloat16 [12288, 2048], P(('path', 'shard')), may hold values from -6 to 6
Outputs:
- master_new: float32 [2, 4096, 2048], P(None, ('path', 'shard'))
- momentum_new: float32 [2, 4096, 2048], P(None, ('path', 'shard'))
Inputs may be any that keep to these rules, and one draw needn't show every extreme that they name: `routes`: every module is read by at least one path.
All inputs are finite; a program needn't handle non-finite values.
Results may differ from a plain program's by a relative error of at most 0.0032.
Values may be sent and summed in bfloat16 or wider, within the bound.
No kernel may reach another device: no remote copies, remote signals or barrier semaphores. Data moves between devices by JAX's collectives and lax.ppermute only.
A program may use at most 128 MiB of HBM per device.

v0:
```python
import jax
import jax.numpy as jnp
from jax import lax
from jax.sharding import PartitionSpec as P


def local(master, momentum, routes, counts, tokens, cotangent):
    path_count = routes.shape[0]
    shards = lax.axis_size("shard")
    modules = master.shape[0]
    rows_block = master.shape[1]
    feat_width = master.shape[2]
    tok_rows = tokens.shape[0]
    model_width = tokens.shape[1]
    inv_root = model_width ** (-0.5)
    chosen = routes[:, 0]
    onehot = (chosen[None, :] == jnp.arange(modules, dtype=jnp.int32)[:, None]).astype(jnp.float32)
    outgoing = jnp.take(master.astype(jnp.bfloat16), chosen, axis=0)
    local_rows = lax.all_to_all(outgoing, "path", split_axis=0, concat_axis=0, tiled=True)
    local_weight = local_rows.reshape(path_count * rows_block, feat_width)
    permuted = tokens.reshape(tok_rows, path_count, shards, rows_block)
    permuted = permuted.transpose(0, 2, 1, 3).reshape(tok_rows, model_width)
    columns = lax.all_to_all(permuted, "shard", split_axis=1, concat_axis=0, tiled=True)
    columns_part = permuted
    pre_sum = jnp.dot(
        columns_part,
        lax.all_gather(local_weight, "shard", axis=0, tiled=True),
        preferred_element_type=jnp.float32,
    )
    pre_act = pre_sum * inv_root
    gate_value = jax.nn.sigmoid(pre_act)
    signal = (
        cotangent.astype(jnp.float32) * gate_value * (1.0 + pre_act * (1.0 - gate_value))
    ).astype(jnp.bfloat16)
    columns_part = columns
    product = lax.dot_general(
        columns_part,
        lax.all_gather(signal, "shard", axis=0, tiled=True),
        (((0,), (0,)), ((), ())),
        preferred_element_type=jnp.float32,
    )
    path_grad = (
        (product * inv_root).astype(jnp.bfloat16).reshape(path_count, rows_block, feat_width)
    )
    received = lax.all_to_all(path_grad, "path", split_axis=0, concat_axis=0, tiled=True)
    mixing = onehot * counts.astype(jnp.float32)[None, :]
    mixing = mixing / jnp.sum(mixing, axis=1, keepdims=True)
    flat_recv = received.reshape(path_count, rows_block * feat_width).astype(jnp.float32)
    outer_grad = jnp.dot(mixing, flat_recv, precision=lax.Precision.HIGHEST).reshape(
        modules, rows_block, feat_width
    )
    momentum_new = 0.9 * momentum + outer_grad
    master_new = master - 0.7 * (outer_grad + 0.9 * momentum_new)
    return (master_new, momentum_new)


def solution(mesh):
    placed = (
        P(None, ("path", "shard"), None),
        P(None, ("path", "shard"), None),
        P(),
        P(),
        P(("path", "shard"), None),
        P(("path", "shard"), None),
    )
    return jax.shard_map(
        local,
        mesh=mesh,
        in_specs=placed,
        out_specs=(P(None, ("path", "shard"), None), P(None, ("path", "shard"), None)),
        check_vma=False,
    )
```

profile of v0, /device:TPU:0, one launch (start us, length us, event | category | flops | bytes accessed | tf_op | source)
XLA Modules:
  0.0 444.9 jit_solution(9973681836863088704)
XLA Ops:
  7.2 0.0 all-gather.3.cloned.1.call-start
  7.2 0.7 fusion.16
  7.9 0.7 and_bitcast_fusion
  8.5 1.7 convert_element_type.22
  10.3 2.8 gather_fusion
  13.0 2.7 broadcast_select_fusion
  15.7 100.3 %all_to_all.29 = bf16[8,128,2048]{2,1,0:T(8,128)(2,1)} all-to-all(bf16[8,128,2048]{2,1,0:T(8,128)(2,1)S(1)} %broadcast_select_fusion), channel_id=1, replica_groups=mesh['path'=8,'shard'=4] {'path'}, dimensions={0} | all-to-all | bytes 8388608 | tf_op jit(solution)/shard_map/all_to_all | solution.py:19
  116.0 0.0 copy-start
  116.0 0.0 all-gather.3.cloned.1.call-update
  116.1 0.0 all-gather.5.cloned.1.call-start
  116.1 1.8 copy-done
  117.9 2.8 copy.27
  120.7 2.7 copy.28
  123.5 2.8 copy.26
  126.3 94.9 %all-gather.3.cloned.1.call-done = bf16[4096,2048]{1,0:T(8,128)(2,1)} async-done(((bf16[1024,2048]{1,0:T(8,128)(2,1)}), bf16[4096,2048]{1,0:T(8,128)(2,1)}) %all-gather.3.cloned.1.call-update) | async-done | bytes 16777232 | tf_op jit(solution)/shard_map/all_gather | solution.py:27
  221.2 14.3 %fusion.5 = bf16[384,2048]{0,1:T(8,128)(2,1)} fusion(bf16[384,2048]{0,1:T(8,128)(2,1)} %copy.26, bf16[4096,2048]{1,0:T(8,128)(2,1)} %all-gather.3.cloned.1.call-done, bf16[384,4096]{0,1:T(8,128)(2,1)S(1)} %bitcast.51), kind=kOutput, calls=%fused_computation.11 | convolution fusion | flops 6451101696 | bytes 23068672 | tf_op jit(solution)/shard_map/dot_general | solution.py:25
  235.5 0.0 all-gather.5.cloned.1.call-update
  235.5 69.7 %all_to_all.30 = bf16[384,4,1024]{0,2,1:T(8,128)(2,1)} all-to-all(bf16[384,4,1024]{0,2,1:T(8,128)(2,1)S(1)} %bitcast.52), channel_id=1, replica_groups=mesh['path'=8,'shard'=4] {'shard'}, dimensions={1} | all-to-all | bytes 6291456 | tf_op jit(solution)/shard_map/all_to_all | solution.py:23
  305.1 3.2 copy.30
  308.4 2.6 all-gather.5.cloned.1.call-done
  311.0 11.1 %multiply_convert_fusion = bf16[2048,1024]{0,1:T(8,128)(2,1)} fusion(bf16[1536,2048]{0,1:T(8,128)(2,1)} %all-gather.5.cloned.1.call-done, bf16[1536,1024]{1,0:T(8,128)(2,1)S(1)} %bitcast.56), kind=kOutput, calls=%fused_computation.1 | convolution fusion | flops 6446645248 | bytes 13631488 | tf_op jit(solution)/shard_map/dot_general | solution.py:36
  322.1 0.0 copy-start.2
  322.1 0.0 copy-start.3
  322.1 5.6 %all-to-all-start.2 = ((bf16[8,128,2048]{2,1,0:T(8,128)(2,1)}), bf16[8,128,2048]{2,1,0:T(8,128)(2,1)}, u32[]{:S(2)}, u32[]{:S(2)}) async-start(bf16[8,128,2048]{2,1,0:T(8,128)(2,1)} %bitcast.55), calls=%async_computation.2 | async-start | bytes 8388608 | tf_op jit(solution)/shard_map/all_to_all | solution.py:45
  327.8 0.0 copy-done.2
  327.8 0.0 copy-done.3
  327.8 0.1 fusion.10
  327.9 93.6 %all-to-all-done.2 = bf16[8,128,2048]{2,1,0:T(8,128)(2,1)} async-done(((bf16[8,128,2048]{2,1,0:T(8,128)(2,1)}), bf16[8,128,2048]{2,1,0:T(8,128)(2,1)}, u32[]{:S(2)}, u32[]{:S(2)}) %all-to-all-start.2) | async-done | bytes 4194336 | tf_op jit(solution)/shard_map/all_to_all | solution.py:45
  421.5 0.0 copy-done.1
  421.5 11.5 %fusion.6 = (f32[2,128,2048]{2,0,1:T(2,128)S(1)}, f32[2,128,2048]{2,0,1:T(2,128)S(1)}) fusion(f32[2,128,2048]{2,1,0:T(8,128)} %param.7, f32[2,128,2048]{2,1,0:T(8,128)S(1)} %copy-done.1, f32[2]{0:T(128)S(1)} %fusion.10, f32[8]{0:T(128)S(1)} %convert_element_type.20, s32[8]{0:T(128)S(1)} %bitcast.58, bf16[1,8,128,2048]{3,2,1,0:T(8,128)(2,1)} %bitcast.19), kind=kOutput, calls=%fused_computation.14 | convolution fusion | flops 53477424 | bytes 12582984 | tf_op jit(solution)/shard_map/dot_general | solution.py:49
  433.0 2.5 copy.33
  435.5 2.5 copy.34
  (3 shorter events, 0.0 us)
Async XLA Ops:
  7.2 214.0 %all-gather.3.cloned.1.call-start = ((), (), s32[]{:S(2)}) async-start(), calls=%async_computation.3 | async-start | bytes 20971520 | tf_op jit(solution)/shard_map/all_gather | solution.py:27
  116.0 1.9 copy-start
  116.1 194.9 %all-gather.5.cloned.1.call-start = ((), (), s32[]{:S(2)}) async-start(), calls=%async_computation.4 | async-start | bytes 7864320 | tf_op jit(solution)/shard_map/all_gather | solution.py:38
  322.1 5.7 %copy-start.2 = (s32[8]{0:T(128)S(1)}, s32[8]{0:T(128)}, u32[]{:S(2)}) copy-start(s32[8]{0:T(128)} %param.9) | copy-start | bytes 100
  322.1 5.7 %copy-start.3 = (s32[8,1]{0,1:T(1,128)S(1)}, s32[8,1]{0,1:T(1,128)}, u32[]{:S(2)}) copy-start(s32[8,1]{0,1:T(1,128)} %param.8) | copy-start | bytes 100
  322.1 99.3 %copy-start.1 = (f32[2,128,2048]{2,1,0:T(8,128)S(1)}, f32[2,128,2048]{2,1,0:T(8,128)}, u32[]{:S(2)}) copy-start(f32[2,128,2048]{2,1,0:T(8,128)} %param.6) | copy-start | bytes 6291460
  322.1 99.3 %all-to-all-start.2 = ((bf16[8,128,2048]{2,1,0:T(8,128)(2,1)}), bf16[8,128,2048]{2,1,0:T(8,128)(2,1)}, u32[]{:S(2)}, u32[]{:S(2)}) async-start(bf16[8,128,2048]{2,1,0:T(8,128)(2,1)} %bitcast.55), calls=%async_computation.2 | async-start | bytes 8388608 | tf_op jit(solution)/shard_map/all_to_all | solution.py:45
Sparse Core Ops, SparseCore 0:
  116.2 104.9 all-gather.2
  235.6 75.3 all-gather.4
where the time goes:
time: 445 us
  waiting for transfers between devices  191 us (43%)
  blocking collectives  170 us (38%)
  matrix products  36.9 us (8%)
  local copies, waits for them, and re-layouts  21.2 us (5%)
  between operations  14.1 us (3%)
  other arithmetic  5.83 us (1%)
  starting transfers between devices  5.72 us (1%)
    all_to_all x1, blocking collectives, local(): lax.all_to_all(outgoing, 'path', split_axis=0, concat_axis=0, tiled=True)  100 us
    all_gather x1, waiting for transfers between devices, local(): lax.all_gather(local_weight, 'shard', axis=0, tiled=True)  94.9 us
    all_to_all x1, waiting for transfers between devices, local(): lax.all_to_all(path_grad, 'path', split_axis=0, concat_axis=0, tiled=True)  93.6 us
    all_to_all x1, blocking collectives, local(): lax.all_to_all(permuted, 'shard', split_axis=1, concat_axis=0, tiled=True)  69.7 us
    dot_general x1, matrix products, local(): jnp.dot(columns_part, lax.all_gather(local_weight, 'shard', axis=0, tiled...  14.3 us
    unnamed x12, local copies, waits for them, and re-layouts  12.5 us
    dot_general x1, matrix products, local(): jnp.dot(mixing, flat_recv, precision=lax.Precision.HIGHEST)  11.5 us
    dot_general x1, matrix products, local(): lax.dot_general(columns_part, lax.all_gather(signal, 'shard', axis=0, til...  11.1 us
  transfers between devices with their start and end apart: 3, of which 3 were waited for; matrix products, arithmetic and copies ran while one was open for 3% of the time, Pallas kernels for 0%

commit v1 on v0

--- a/solution.py
+++ b/solution.py
@@ -20,7 +20,11 @@
     local_weight = local_rows.reshape(path_count * rows_block, feat_width)
     permuted = tokens.reshape(tok_rows, path_count, shards, rows_block)
     permuted = permuted.transpose(0, 2, 1, 3).reshape(tok_rows, model_width)
-    columns = lax.all_to_all(permuted, "shard", split_axis=1, concat_axis=0, tiled=True)
+    moved = jax.lax.axis_size("shard")
+    a_next = jnp.split(permuted, moved, axis=1)
+    field_out = jnp.stack(a_next)
+    extra = jax.lax.all_to_all(field_out, "shard", split_axis=0, concat_axis=0)
+    columns = jnp.concatenate(extra, axis=0)
     columns_part = permuted
     pre_sum = jnp.dot(
         columns_part,

time: 445 us -> 446 us (level)
  no operation moved by 1% of the time
where the time goes in v1:
time: 446 us; the launch traced here: 445 us
  waiting for transfers between devices  193 us (43%)
  blocking collectives  169 us (38%)
  matrix products  37 us (8%)
  local copies, waits for them, and re-layouts  19.4 us (4%)
  between operations  14.1 us (3%)
  other arithmetic  6.37 us (1%)
  starting transfers between devices  5.74 us (1%)
    all_to_all x1, blocking collectives, local(): lax.all_to_all(outgoing, 'path', split_axis=0, concat_axis=0, tiled=True)  100 us
    all_gather x1, waiting for transfers between devices, local(): lax.all_gather(local_weight, 'shard', axis=0, tiled=True)  96.8 us
    all_to_all x1, waiting for transfers between devices, local(): lax.all_to_all(path_grad, 'path', split_axis=0, concat_axis=0, tiled=True)  93.6 us
    all_to_all x1, blocking collectives, local(): extra = jax.lax.all_to_all(field_out, 'shard', split_axis=0, concat_axis=0)  69 us
    dot_general x1, matrix products, local(): jnp.dot(columns_part, lax.all_gather(local_weight, 'shard', axis=0, tiled...  14.3 us
    dot_general x1, matrix products, local(): jnp.dot(mixing, flat_recv, precision=lax.Precision.HIGHEST)  11.5 us
    dot_general x1, matrix products, local(): lax.dot_general(columns_part, lax.all_gather(signal, 'shard', axis=0, til...  11.2 us
    unnamed x12, local copies, waits for them, and re-layouts  10.6 us
  transfers between devices with their start and end apart: 3, of which 3 were waited for; matrix products, arithmetic and copies ran while one was open for 3% of the time, Pallas kernels for 0%

profile of v1, /device:TPU:0, one launch (start us, length us, event | category | flops | bytes accessed | tf_op | source)
XLA Modules:
  0.0 445.1 jit_solution(12896222260024950243)
XLA Ops:
  7.2 0.0 all-gather.3.cloned.1.call-start
  7.2 0.7 and_bitcast_fusion
  7.9 0.7 fusion.16
  8.5 1.7 convert_element_type.19
  10.3 2.8 gather_fusion
  13.0 2.7 broadcast_select_fusion
  15.7 100.3 %all_to_all.15 = bf16[8,128,2048]{2,1,0:T(8,128)(2,1)} all-to-all(bf16[8,128,2048]{2,1,0:T(8,128)(2,1)S(1)} %broadcast_select_fusion), channel_id=1, replica_groups=mesh['path'=8,'shard'=4] {'path'}, dimensions={0} | all-to-all | bytes 8388608 | tf_op jit(solution)/shard_map/all_to_all | solution.py:19
  116.0 0.0 all-gather.3.cloned.1.call-update
  116.1 0.0 all-gather.5.cloned.1.call-start
  116.1 2.7 copy.21
  118.9 0.0 copy-done
  118.9 2.8 copy.18
  121.6 2.7 copy.19
  124.4 96.8 %all-gather.3.cloned.1.call-done = bf16[4096,2048]{1,0:T(8,128)(2,1)} async-done(((bf16[1024,2048]{1,0:T(8,128)(2,1)}), bf16[4096,2048]{1,0:T(8,128)(2,1)}) %all-gather.3.cloned.1.call-update) | async-done | bytes 16777232 | tf_op jit(solution)/shard_map/all_gather | solution.py:31
  221.2 14.3 %fusion.5 = bf16[384,2048]{0,1:T(8,128)(2,1)} fusion(bf16[384,2048]{0,1:T(8,128)(2,1)} %copy.21, bf16[4096,2048]{1,0:T(8,128)(2,1)} %all-gather.3.cloned.1.call-done, bf16[384,4096]{0,1:T(8,128)(2,1)S(1)} %bitcast.55), kind=kOutput, calls=%fused_computation.12 | convolution fusion | flops 6451101696 | bytes 23068672 | tf_op jit(solution)/shard_map/dot_general | solution.py:29
  235.5 0.0 all-gather.5.cloned.1.call-update
  235.5 0.3 slice_bitcast_fusion.3
  235.8 0.5 pad_maximum_fusion
  236.4 69.0 %all_to_all.16 = bf16[4,384,1024]{1,2,0:T(8,128)(2,1)S(1)} all-to-all(bf16[4,384,1024]{1,2,0:T(8,128)(2,1)S(1)} %pad_maximum_fusion), channel_id=1, replica_groups=mesh['path'=8,'shard'=4] {'shard'}, dimensions={0} | all-to-all | bytes 6291456 | tf_op jit(solution)/shard_map/all_to_all | solution.py:26
  305.3 2.9 copy.20
  308.3 2.9 all-gather.5.cloned.1.call-done
  311.1 11.2 %multiply_convert_fusion = bf16[1024,2048]{1,0:T(8,128)(2,1)} fusion(bf16[1536,1024]{1,0:T(8,128)(2,1)} %bitcast.59, bf16[1536,2048]{0,1:T(8,128)(2,1)} %all-gather.5.cloned.1.call-done), kind=kOutput, calls=%fused_computation.1 | convolution fusion | flops 6446645248 | bytes 13631488 | tf_op jit(solution)/shard_map/dot_general | solution.py:40
  322.3 0.0 copy-start.2
  322.3 5.7 %all-to-all-start.2 = ((bf16[8,128,2048]{2,1,0:T(8,128)(2,1)}), bf16[8,128,2048]{2,1,0:T(8,128)(2,1)}, u32[]{:S(2)}, u32[]{:S(2)}) async-start(bf16[8,128,2048]{2,1,0:T(8,128)(2,1)} %bitcast.58), calls=%async_computation.2 | async-start | bytes 8388608 | tf_op jit(solution)/shard_map/all_to_all | solution.py:49
  328.0 0.0 copy-done.2
  328.0 0.0 copy-done.3
  328.0 0.1 fusion.10
  328.1 93.6 %all-to-all-done.2 = bf16[8,128,2048]{2,1,0:T(8,128)(2,1)} async-done(((bf16[8,128,2048]{2,1,0:T(8,128)(2,1)}), bf16[8,128,2048]{2,1,0:T(8,128)(2,1)}, u32[]{:S(2)}, u32[]{:S(2)}) %all-to-all-start.2) | async-done | bytes 4194336 | tf_op jit(solution)/shard_map/all_to_all | solution.py:49
  421.7 0.0 copy-done.1
  421.7 11.5 %fusion.6 = (f32[2,128,2048]{2,0,1:T(2,128)S(1)}, f32[2,128,2048]{2,0,1:T(2,128)S(1)}) fusion(f32[2,128,2048]{2,1,0:T(8,128)} %param.7, f32[2,128,2048]{2,1,0:T(8,128)S(1)} %copy-done.1, f32[2]{0:T(128)S(1)} %fusion.10, f32[8]{0:T(128)S(1)} %convert_element_type.17, s32[8]{0:T(128)S(1)} %bitcast.61, bf16[1,8,128,2048]{3,2,1,0:T(8,128)(2,1)} %bitcast.19), kind=kOutput, calls=%fused_computation.15 | convolution fusion | flops 53477424 | bytes 12582984 | tf_op jit(solution)/shard_map/dot_general | solution.py:53
  433.2 2.5 copy.25
  435.7 2.5 copy.24
  (5 shorter events, 0.0 us)
Async XLA Ops:
  7.2 214.0 %all-gather.3.cloned.1.call-start = ((), (), s32[]{:S(2)}) async-start(), calls=%async_computation.3 | async-start | bytes 20971520 | tf_op jit(solution)/shard_map/all_gather | solution.py:31
  116.0 2.8 copy-start
  116.1 195.0 %all-gather.5.cloned.1.call-start = ((), (), s32[]{:S(2)}) async-start(), calls=%async_computation.4 | async-start | bytes 7864320 | tf_op jit(solution)/shard_map/all_gather | solution.py:42
  322.3 5.7 %copy-start.2 = (s32[8]{0:T(128)S(1)}, s32[8]{0:T(128)}, u32[]{:S(2)}) copy-start(s32[8]{0:T(128)} %param.9) | copy-start | bytes 100
  322.3 5.7 %copy-start.3 = (s32[8,1]{0,1:T(1,128)S(1)}, s32[8,1]{0,1:T(1,128)}, u32[]{:S(2)}) copy-start(s32[8,1]{0,1:T(1,128)} %param.8) | copy-start | bytes 100
  322.3 99.4 %copy-start.1 = (f32[2,128,2048]{2,1,0:T(8,128)S(1)}, f32[2,128,2048]{2,1,0:T(8,128)}, u32[]{:S(2)}) copy-start(f32[2,128,2048]{2,1,0:T(8,128)} %param.6) | copy-start | bytes 6291460
  322.3 99.4 %all-to-all-start.2 = ((bf16[8,128,2048]{2,1,0:T(8,128)(2,1)}), bf16[8,128,2048]{2,1,0:T(8,128)(2,1)}, u32[]{:S(2)}, u32[]{:S(2)}) async-start(bf16[8,128,2048]{2,1,0:T(8,128)(2,1)} %bitcast.58), calls=%async_computation.2 | async-start | bytes 8388608 | tf_op jit(solution)/shard_map/all_to_all | solution.py:49
Sparse Core Ops, SparseCore 0:
  116.2 104.9 all-gather.2
  235.6 75.4 all-gather.4
